TPU v7x, 256 devices: a whole 4x4x8 slice. The times are simulated.
256 devices in a mesh: seq: 8 (over z_hi, core), req: 32 (over x, z_lo, y).
Axes of the slice: x: 4, y: 4, z: 8 (z_hi: 4, z_lo: 2; z = z_hi * 2 + z_lo), core: 2. Of those that a mesh axis runs over, the one named last changes fastest.
Arguments:
- inputs: bfloat16 [32, 16, 4, 1536], P('req', 'seq'), may hold values from -6 to 6
- parents: int32 [32, 4, 16], P('req'), may hold values from 0 to 15
- block_len: int32 [32, 128], P('req', 'seq'), may hold values from 0 to 128, as said below
- prompt_key_cache: bfloat16 [32, 16384, 512], P('req', 'seq'), may hold values from -230 to 230
- prompt_value_cache: bfloat16 [32, 16384, 512], P('req', 'seq'), may hold values from -6 to 6
- generated_key_cache: bfloat16 [32, 16, 16, 512], P('req', 'seq'), may hold values from -6 to 6
- generated_value_cache: bfloat16 [32, 16, 16, 512], P('req', 'seq'), may hold values from -6 to 6
- gain_attn: float32 [1536], replicated, may hold values from 0.1 to 1.9
- gain_moe: float32 [1536], replicated, may hold values from 0.1 to 1.9
- w_query: bfloat16 [1536, 1536], P(None, 'seq'), may hold values from -0.15625 to 0.15625
- key_projection_weight: bfloat16 [1536, 512], P(None, 'seq'), may hold values from -0.15625 to 0.15625
- value_projection_weight: bfloat16 [1536, 512], P(None, 'seq'), may hold values from -0.15625 to 0.15625
- w_output: bfloat16 [1536, 1536], P('seq'), may hold values from -0.15625 to 0.15625
- w_in: bfloat16 [32, 1536, 1024], P('req'), may hold values from -0.15625 to 0.15625
- w_out: bfloat16 [32, 512, 1536], P('req'), may hold values from -0.25 to 0.25
- routes: int32 [32, 16, 4, 8], P('req', 'seq'), may hold values from 0 to 31, all different within a row; in each aligned block of 8 rows (0 to 7, 8 to 15, ..., all dimensions but the last counted through in order) at most 4 rows name the same one
- gate_weights: float32 [32, 16, 4, 8], P('req', 'seq'), may hold values from 0.05 to 1
Outputs:
- mixed: bfloat16 [32, 16, 4, 1536], P('req', 'seq')
- final_k: bfloat16 [32, 16, 20, 512], P('req', 'seq')
- final_v: bfloat16 [32, 16, 20, 512], P('req', 'seq')
Inputs may be any that keep to these rules, and one draw needn't show every extreme that they name: block_len[r, j] is the number of live positions at the start of block j of request r; 0 marks an empty block; the first block of every request is full. `routes`: among the rows of one device (its 2 beams over all 4 steps, in the order beam then step) no expert is named more than 4 times.
All inputs are finite; a program needn't handle non-finite values.
Results may differ from a plain program's by a relative error of at most 0.025.
Values may be sent and summed in bfloat16 or wider, within the bound.
No kernel may reach another device: no remote copies, remote signals or barrier semaphores. Data moves between devices by JAX's collectives and lax.ppermute only.
A program may use at most 128 MiB of HBM per device.

v0:
```python
from functools import reduce
import jax
import jax.numpy as jnp
from jax import lax
from jax.sharding import PartitionSpec as P

QUERY_HEADS = 24
HEAD_SIZE = 64
BLK = 128
EPSILON = 1e-05
ROPE_BASE = 10000.0
NEGATIVE_FILL = -1e30
SCORE_SCALE = 0.125


def merged(x, axis, join):
    gathered = jax.tree.map(
        lambda a, kind: lax.all_gather(a.astype(kind), axis),
        x,
        jax.tree.map(lambda a: jnp.bfloat16 if a.dtype == jnp.float32 else a.dtype, x),
    )

    def take(source):
        return jax.tree.map(
            lambda a, own: lax.dynamic_index_in_dim(a, source, 0, False).astype(own.dtype),
            gathered,
            x,
        )

    return lax.fori_loop(
        1, lax.axis_size(axis), lambda source, state: join(state, take(source)), take(0)
    )


def rms_scale(values, gain_vector):
    values = values.astype(jnp.float32)
    mean_sq = jnp.mean(values * values, axis=-1, keepdims=True)
    return values * lax.rsqrt(mean_sq + EPSILON) * gain_vector


def apply_rotary(values, token_positions, head_dim):
    lead_shape = values.shape[:-1]
    head_count = values.shape[-1] // head_dim
    shaped = values.reshape(lead_shape + (head_count, head_dim))
    half_dim = head_dim // 2
    frequency = ROPE_BASE ** (-(jnp.arange(half_dim, dtype=jnp.float32) * 2.0 / head_dim))
    angles = token_positions[:, None] * frequency[None, :]
    cosine = jnp.cos(angles)[None, :, None, :]
    sine_part = jnp.sin(angles)[None, :, None, :]
    first_half = shaped[..., :half_dim]
    second = shaped[..., half_dim:]
    turned = jnp.concatenate(
        [first_half * cosine - second * sine_part, second * cosine + first_half * sine_part],
        axis=-1,
    )
    return turned.reshape(values.shape)


def project(row_block, weight):
    flattened_rows = row_block.reshape(-1, row_block.shape[-1])
    result = jnp.dot(flattened_rows, weight, preferred_element_type=jnp.float32)
    return result.reshape(row_block.shape[:-1] + (weight.shape[1],))


def local_partial(decode_query_step, pieces):
    scored = []
    for key_rows, values, live in pieces:
        shaped_keys = key_rows.reshape(
            key_rows.shape[0], decode_query_step.shape[1], decode_query_step.shape[3]
        )
        scores = (
            jnp.einsum(
                "bgjd,kgd->bgjk", decode_query_step, shaped_keys, preferred_element_type=jnp.float32
            )
            * SCORE_SCALE
        )
        mask = live[:, None, None, :]
        scored.append(
            (jnp.where(mask, scores, NEGATIVE_FILL), mask, values.reshape(shaped_keys.shape))
        )
    row_max = reduce(jnp.maximum, [jnp.max(entry[0], axis=-1) for entry in scored])
    denominator = jnp.zeros(row_max.shape, jnp.float32)
    numerator = jnp.zeros(row_max.shape + (decode_query_step.shape[3],), jnp.float32)
    for entry in scored:
        weights = jnp.where(entry[1], jnp.exp(entry[0] - row_max[..., None]), 0.0)
        denominator = denominator + jnp.sum(weights, axis=-1)
        numerator = numerator + jnp.einsum(
            "bgjk,kgd->bgjd",
            weights.astype(jnp.bfloat16),
            entry[2],
            preferred_element_type=jnp.float32,
        )
    return (row_max, denominator, numerator)


def join_partials(first_part, second_part):
    row_max = jnp.maximum(first_part[0], second_part[0])
    first_scale = jnp.exp(first_part[0] - row_max)
    second_scale = jnp.exp(second_part[0] - row_max)
    denominator = first_scale * first_part[1] + second_scale * second_part[1]
    numerator = first_scale[..., None] * first_part[2] + second_scale[..., None] * second_part[2]
    return (row_max, denominator, numerator)


def expert_block(received, w_in, w_out):
    half_dim = w_out.shape[1]
    projected = jnp.einsum("nesd,edf->nesf", received, w_in, preferred_element_type=jnp.float32)
    activation = (jax.nn.silu(projected[..., :half_dim]) * projected[..., half_dim:]).astype(
        jnp.bfloat16
    )
    return jnp.einsum(
        "nesf,efd->nesd", activation, w_out, preferred_element_type=jnp.float32
    ).astype(jnp.bfloat16)


def route_rows(expert_in, route_ids, pair_weights, capacity, dev_count, experts_all, send_rows):
    row_count, top_count = route_ids.shape
    pair_count = row_count * top_count
    chosen = route_ids.reshape(pair_count)
    pair_index = jnp.arange(pair_count, dtype=jnp.int32)
    before = (chosen[:, None] == chosen[None, :]) & (pair_index[None, :] < pair_index[:, None])
    slot_rank = jnp.sum(before.astype(jnp.int32), axis=1)
    slot_index = chosen * capacity + slot_rank
    slot_table = (
        slot_index[:, None] == jnp.arange(experts_all * capacity, dtype=jnp.int32)[None, :]
    ).astype(jnp.float32)
    row_table = (
        (pair_index // top_count)[:, None] == jnp.arange(row_count, dtype=jnp.int32)[None, :]
    ).astype(jnp.float32)
    placing = jnp.dot(slot_table.T, row_table, precision=lax.Precision.HIGHEST)
    buffer = jnp.dot(
        placing.astype(jnp.bfloat16), expert_in, preferred_element_type=jnp.float32
    ).astype(jnp.bfloat16)
    buffer = buffer.reshape(dev_count, experts_all // dev_count, capacity, expert_in.shape[1])
    returned = send_rows(buffer).reshape(experts_all * capacity, expert_in.shape[1])
    mixing = jnp.dot(
        row_table.T * pair_weights.reshape(pair_count)[None, :],
        slot_table,
        precision=lax.Precision.HIGHEST,
    )
    return jnp.dot(mixing, returned.astype(jnp.float32), precision=lax.Precision.HIGHEST)


def local(
    inputs,
    parents,
    block_len,
    prompt_key_cache,
    prompt_value_cache,
    generated_key_cache,
    generated_value_cache,
    gain_attn,
    gain_moe,
    w_query,
    key_projection_weight,
    value_projection_weight,
    w_output,
    w_in,
    w_out,
    routes,
    gate_weights,
):
    rows_here = inputs.shape[1]
    step_count = inputs.shape[2]
    model_width = inputs.shape[3]
    seq_count = lax.axis_size("seq")
    my_seq = lax.axis_index("seq")
    req_count = lax.axis_size("req")
    experts_all = w_in.shape[0] * req_count
    beam_count = rows_here * seq_count
    prefix_len = prompt_key_cache.shape[1]
    tail_len = generated_key_cache.shape[2]
    kv_width = prompt_key_cache.shape[2]
    kv_heads = kv_width // HEAD_SIZE
    group_size = QUERY_HEADS // kv_heads
    token_positions = jnp.arange(step_count, dtype=jnp.float32) + (
        prefix_len * seq_count + tail_len
    )
    normed = rms_scale(inputs[0], gain_attn).astype(jnp.bfloat16)
    normed_all = lax.all_gather(normed, "seq", axis=0, tiled=True)
    query_rows = apply_rotary(project(normed_all, w_query), token_positions, HEAD_SIZE).astype(
        jnp.bfloat16
    )
    updated_keys = apply_rotary(
        project(normed_all, key_projection_weight), token_positions, HEAD_SIZE
    ).astype(jnp.bfloat16)
    updated_values = project(normed_all, value_projection_weight).astype(jnp.bfloat16)
    queries_all = lax.all_gather(query_rows, "seq", axis=2, tiled=True)
    entry_k, entry_v = (
        lax.all_to_all(updated_keys, "seq", split_axis=0, concat_axis=2, tiled=True),
        lax.all_to_all(updated_values, "seq", split_axis=0, concat_axis=2, tiled=True),
    )
    block_count = block_len.shape[1]
    prefix_live = (jnp.arange(BLK, dtype=jnp.int32)[None, :] < block_len[0][:, None]).reshape(
        1, block_count * BLK
    )
    own_ids = my_seq * rows_here + jnp.arange(rows_here, dtype=jnp.int32)
    beam_ids = jnp.arange(beam_count, dtype=jnp.int32)
    tail_owner = (own_ids[:, None] + jnp.zeros((1, tail_len), jnp.int32)).reshape(
        rows_here * tail_len
    )
    fresh_owner = (own_ids[:, None] + jnp.zeros((1, step_count), jnp.int32)).reshape(
        rows_here * step_count
    )
    fresh_step = (
        jnp.zeros((rows_here, 1), jnp.int32) + jnp.arange(step_count, dtype=jnp.int32)[None, :]
    ).reshape(rows_here * step_count)
    my_parents = lax.dynamic_slice_in_dim(parents[0], my_seq * rows_here, rows_here, 1)
    head_width = w_output.shape[0]

    def send_batch(buffer):
        return lax.all_to_all(
            expert_block(
                lax.all_to_all(buffer, "req", split_axis=0, concat_axis=0, tiled=True), w_in, w_out
            ),
            "req",
            split_axis=0,
            concat_axis=0,
            tiled=True,
        )

    beam_key_cache = generated_key_cache[0]
    beam_value_cache = generated_value_cache[0]
    newest_key = jnp.zeros((rows_here, step_count, kv_width), jnp.bfloat16)
    newest_value = jnp.zeros((rows_here, step_count, kv_width), jnp.bfloat16)
    hidden_rows = []
    for decode_step_index in range(step_count):
        chosen_rows = my_parents[decode_step_index]
        received = (
            lax.all_gather(beam_key_cache, "seq", axis=0, tiled=True),
            lax.all_gather(beam_value_cache, "seq", axis=0, tiled=True),
            lax.all_gather(newest_key, "seq", axis=0, tiled=True),
            lax.all_gather(newest_value, "seq", axis=0, tiled=True),
        )
        beam_key_cache = jnp.take(received[0], chosen_rows, axis=0)
        beam_value_cache = jnp.take(received[1], chosen_rows, axis=0)
        newest_key = jnp.take(received[2], chosen_rows, axis=0)
        newest_value = jnp.take(received[3], chosen_rows, axis=0)
        newest_key = newest_key.at[:, decode_step_index].set(entry_k[:, decode_step_index])
        newest_value = newest_value.at[:, decode_step_index].set(entry_v[:, decode_step_index])
        decode_query_step = queries_all[:, decode_step_index].reshape(
            beam_count, kv_heads, group_size, HEAD_SIZE
        )
        tail_live = beam_ids[:, None] == tail_owner[None, :]
        fresh_live = (beam_ids[:, None] == fresh_owner[None, :]) & (
            fresh_step[None, :] <= decode_step_index
        )
        pieces = [
            (prompt_key_cache[0], prompt_value_cache[0], prefix_live),
            (
                beam_key_cache.reshape(rows_here * tail_len, kv_width),
                beam_value_cache.reshape(rows_here * tail_len, kv_width),
                tail_live,
            ),
            (
                newest_key.reshape(rows_here * step_count, kv_width),
                newest_value.reshape(rows_here * step_count, kv_width),
                fresh_live,
            ),
        ]
        partial_state = local_partial(decode_query_step, pieces)
        row_max, denominator, numerator = merged(partial_state, "seq", join_partials)
        attended_heads = (
            (numerator / denominator[..., None])
            .reshape(beam_count, QUERY_HEADS * HEAD_SIZE)
            .astype(jnp.bfloat16)
        )
        own_heads = lax.dynamic_slice_in_dim(attended_heads, my_seq * head_width, head_width, 1)
        attended = lax.psum_scatter(
            jnp.dot(own_heads, w_output, preferred_element_type=jnp.float32).astype(jnp.bfloat16),
            "seq",
            scatter_dimension=0,
            tiled=True,
        ).astype(jnp.float32)
        hidden = inputs[0][:, decode_step_index].astype(jnp.float32) + attended
        hidden_rows.append(hidden)
    stacked = jnp.stack(hidden_rows, axis=1).reshape(rows_here * step_count, model_width)
    expert_in = rms_scale(stacked, gain_moe).astype(jnp.bfloat16)
    capacity = 2 * rows_here * step_count * routes.shape[3] // experts_all
    route_ids = routes[0].reshape(rows_here * step_count, routes.shape[3])
    pair_weights = gate_weights[0].reshape(rows_here * step_count, routes.shape[3])
    summed = route_rows(
        expert_in, route_ids, pair_weights, capacity, req_count, experts_all, send_batch
    )
    mixed = (stacked + summed).astype(jnp.bfloat16).reshape(rows_here, step_count, model_width)
    final_k = jnp.concatenate([beam_key_cache, newest_key], axis=1)
    final_v = jnp.concatenate([beam_value_cache, newest_value], axis=1)
    return (mixed[None], final_k[None], final_v[None])


def solution(mesh):
    placed = (
        P("req", "seq", None, None),
        P("req", None, None),
        P("req", "seq"),
        P("req", "seq", None),
        P("req", "seq", None),
        P("req", "seq", None, None),
        P("req", "seq", None, None),
        P(),
        P(),
        P(None, "seq"),
        P(None, "seq"),
        P(None, "seq"),
        P("seq", None),
        P("req", None, None),
        P("req", None, None),
        P("req", "seq", None, None),
        P("req", "seq", None, None),
    )
    return jax.shard_map(
        local,
        mesh=mesh,
        in_specs=placed,
        out_specs=(
            P("req", "seq", None, None),
            P("req", "seq", None, None),
            P("req", "seq", None, None),
        ),
        check_vma=False,
    )
```

profile of v0, /device:TPU:8, one launch (start us, length us, event | category | flops | bytes accessed | tf_op | source)
XLA Modules:
  0.0 895.3 jit_solution(18292231915327274517)
XLA Ops:
  9.3 18.2 %all_gather.108 = bf16[16,4,1536]{2,1,0:T(4,128)(2,1)S(1)} all-gather(bf16[2,4,1536]{2,1,0:T(4,128)(2,1)S(1)} %fusion.149), channel_id=1, replica_groups=mesh['seq'=8,'req'=32] {'seq'}, dimensions={0}, use_global_device_ids=true | all-gather | bytes 221184 | tf_op jit(solution)/shard_map/all_gather | solution.py:180
  29.6 4.8 all-to-all-start
  38.5 18.3 %all-gather.3 = bf16[1,16,16,512]{3,2,0,1:T(8,128)(2,1)} all-gather(bf16[1,2,16,512]{3,2,0,1:T(8,128)(2,1)} %bitcast.429), channel_id=5, replica_groups=mesh['seq'=8,'req'=32] {'seq'}, dimensions={1}, use_global_device_ids=true | all-gather | bytes 294912 | tf_op jit(solution)/shard_map/all_gather | solution.py:231
  56.8 16.0 %all-gather = bf16[1,16,16,512]{3,2,0,1:T(8,128)(2,1)} all-gather(bf16[1,2,16,512]{3,2,0,1:T(8,128)(2,1)} %bitcast.430), channel_id=2, replica_groups=mesh['seq'=8,'req'=32] {'seq'}, dimensions={1}, use_global_device_ids=true | all-gather | bytes 294912 | tf_op jit(solution)/shard_map/all_gather | solution.py:230
  75.9 15.7 %all_gather.117 = bf16[16,16,512]{2,1,0:T(8,128)(2,1)} all-gather(bf16[2,16,512]{2,1,0:T(8,128)(2,1)S(1)} %get-tuple-element.1075), channel_id=1, replica_groups=mesh['seq'=8,'req'=32] {'seq'}, dimensions={0}, use_global_device_ids=true | all-gather | bytes 294912 | tf_op jit(solution)/shard_map/all_gather | solution.py:230
  92.3 15.7 %all_gather.121 = bf16[16,16,512]{2,1,0:T(8,128)(2,1)} all-gather(bf16[2,16,512]{2,1,0:T(8,128)(2,1)S(1)} %get-tuple-element.1074), channel_id=1, replica_groups=mesh['seq'=8,'req'=32] {'seq'}, dimensions={0}, use_global_device_ids=true | all-gather | bytes 294912 | tf_op jit(solution)/shard_map/all_gather | solution.py:231
  111.2 15.7 %all_gather.125 = bf16[16,16,512]{2,1,0:T(8,128)(2,1)} all-gather(bf16[2,16,512]{2,1,0:T(8,128)(2,1)S(1)} %get-tuple-element.1073), channel_id=1, replica_groups=mesh['seq'=8,'req'=32] {'seq'}, dimensions={0}, use_global_device_ids=true | all-gather | bytes 294912 | tf_op jit(solution)/shard_map/all_gather | solution.py:230
  127.6 15.7 %all_gather.129 = bf16[16,16,512]{2,1,0:T(8,128)(2,1)} all-gather(bf16[2,16,512]{2,1,0:T(8,128)(2,1)S(1)} %get-tuple-element.1072), channel_id=1, replica_groups=mesh['seq'=8,'req'=32] {'seq'}, dimensions={0}, use_global_device_ids=true | all-gather | bytes 294912 | tf_op jit(solution)/shard_map/all_gather | solution.py:231
  147.0 15.7 %all_gather.133 = bf16[16,16,512]{2,1,0:T(8,128)(2,1)} all-gather(bf16[2,16,512]{2,1,0:T(8,128)(2,1)S(1)} %get-tuple-element.1071), channel_id=1, replica_groups=mesh['seq'=8,'req'=32] {'seq'}, dimensions={0}, use_global_device_ids=true | all-gather | bytes 294912 | tf_op jit(solution)/shard_map/all_gather | solution.py:230
  167.3 20.3 %all_gather.109 = bf16[16,4,1536]{0,1,2:T(4,128)(2,1)S(1)} all-gather(bf16[16,4,192]{0,1,2:T(4,128)(2,1)S(1)} %bitcast.396), channel_id=1, replica_groups=mesh['seq'=8,'req'=32] {'seq'}, dimensions={2}, use_global_device_ids=true | all-gather | bytes 221184 | tf_op jit(solution)/shard_map/all_gather | solution.py:188
  187.6 3.6 fusion.236
  191.2 2.1 copy.343
  196.4 1.7 convolution_convert_fusion.6
  205.1 3.9 copy.275
  209.1 16.2 %all_gather.137 = bf16[16,16,512]{2,1,0:T(8,128)(2,1)} all-gather(bf16[2,16,512]{2,1,0:T(8,128)(2,1)S(1)} %copy-done.31), channel_id=1, replica_groups=mesh['seq'=8,'req'=32] {'seq'}, dimensions={0}, use_global_device_ids=true | all-gather | bytes 294912 | tf_op jit(solution)/shard_map/all_gather | solution.py:231
  229.3 2.1 copy.274
  231.6 4.7 bitcast_reduce_fusion
  236.3 3.0 bitcast_reduce_fusion.3
  242.3 2.1 copy.304
  244.5 4.7 bitcast_reduce_fusion.2
  250.7 2.7 copy.324
  255.1 4.8 bitcast_reduce_fusion.1
  265.9 3.9 copy.287
  271.8 4.9 all-to-all-start.1
  277.7 16.9 %all_gather.118 = bf16[16,4,512]{2,1,0:T(4,128)(2,1)S(1)} all-gather(bf16[2,4,512]{2,1,0:T(4,128)(2,1)S(1)} %scatter.26), channel_id=1, replica_groups=mesh['seq'=8,'req'=32] {'seq'}, dimensions={0}, use_global_device_ids=true | all-gather | bytes 73728 | tf_op jit(solution)/shard_map/all_gather | solution.py:232
  295.5 14.5 %all_gather.122 = bf16[16,4,512]{2,1,0:T(4,128)(2,1)S(1)} all-gather(bf16[2,4,512]{2,1,0:T(4,128)(2,1)S(1)} %scatter.29), channel_id=1, replica_groups=mesh['seq'=8,'req'=32] {'seq'}, dimensions={0}, use_global_device_ids=true | all-gather | bytes 73728 | tf_op jit(solution)/shard_map/all_gather | solution.py:233
  312.3 14.5 %all_gather.126 = bf16[16,4,512]{2,1,0:T(4,128)(2,1)S(1)} all-gather(bf16[2,4,512]{2,1,0:T(4,128)(2,1)S(1)} %scatter.30), channel_id=1, replica_groups=mesh['seq'=8,'req'=32] {'seq'}, dimensions={0}, use_global_device_ids=true | all-gather | bytes 73728 | tf_op jit(solution)/shard_map/all_gather | solution.py:232
  326.9 14.6 %all_gather.130 = bf16[16,4,512]{2,1,0:T(4,128)(2,1)S(1)} all-gather(bf16[2,4,512]{2,1,0:T(4,128)(2,1)S(1)} %scatter.31), channel_id=1, replica_groups=mesh['seq'=8,'req'=32] {'seq'}, dimensions={0}, use_global_device_ids=true | all-gather | bytes 73728 | tf_op jit(solution)/shard_map/all_gather | solution.py:233
  343.6 14.6 %all_gather.134 = bf16[16,4,512]{2,1,0:T(4,128)(2,1)S(1)} all-gather(bf16[2,4,512]{2,1,0:T(4,128)(2,1)S(1)} %scatter.34), channel_id=1, replica_groups=mesh['seq'=8,'req'=32] {'seq'}, dimensions={0}, use_global_device_ids=true | all-gather | bytes 73728 | tf_op jit(solution)/shard_map/all_gather | solution.py:232
  358.3 14.5 %all_gather.138 = bf16[16,4,512]{2,1,0:T(4,128)(2,1)S(1)} all-gather(bf16[2,4,512]{2,1,0:T(4,128)(2,1)S(1)} %scatter.35), channel_id=1, replica_groups=mesh['seq'=8,'req'=32] {'seq'}, dimensions={0}, use_global_device_ids=true | all-gather | bytes 73728 | tf_op jit(solution)/shard_map/all_gather | solution.py:233
  378.2 1.8 fusion.242
  380.1 1.8 fusion.244
  381.9 2.0 fusion.246
  386.6 4.0 fusion.81
  394.8 3.0 fusion.23
  399.3 14.6 %all-gather.11 = bf16[128,8,3]{1,2,0:T(4,128)(2,1)S(1)} all-gather(bf16[16,8,3]{1,2,0:T(4,128)(2,1)S(1)} %copy.349), channel_id=13, replica_groups=mesh['seq'=8,'req'=32] {'seq'}, dimensions={0}, use_global_device_ids=true | all-gather | bytes 6912 | tf_op jit(solution)/shard_map/all_gather | solution.py:18
  415.4 2.3 fusion.106
  418.5 14.6 %all-gather.12 = bf16[128,8,3]{1,2,0:T(4,128)(2,1)S(1)} all-gather(bf16[16,8,3]{1,2,0:T(4,128)(2,1)S(1)} %copy.350), channel_id=14, replica_groups=mesh['seq'=8,'req'=32] {'seq'}, dimensions={0}, use_global_device_ids=true | all-gather | bytes 6912 | tf_op jit(solution)/shard_map/all_gather | solution.py:18
  438.1 15.3 %all-gather.13 = bf16[128,8,3,64]{3,0,2,1:T(8,128)(2,1)S(1)} all-gather(bf16[16,8,3,64]{3,0,2,1:T(8,128)(2,1)S(1)} %fusion.87), channel_id=15, replica_groups=mesh['seq'=8,'req'=32] {'seq'}, dimensions={0}, use_global_device_ids=true | all-gather | bytes 442368 | tf_op jit(solution)/shard_map/all_gather | solution.py:18
  457.7 33.8 %while.87 = (s32[]{:T(128)}, f32[16,8,3]{0,1,2:T(8,128)S(1)}, f32[16,8,3]{0,1,2:T(8,128)S(1)}, f32[16,8,3,64]{3,2,1,0:T(4,128)S(1)}, bf16[8,16,8,3]{1,2,3,0:T(8,...) while((s32[]{:T(128)}, f32[16,8,3]{0,1,2:T(8,128)S(1)}, ...), condition=%wide.region_35.38_spmd, body=%wide.region_34.37_spmd.sunk | while | flops 101381 | bytes 364183 | solution.py:30
  460.9 1.7 fusion.279
  475.3 1.7 fusion.279
  480.2 1.7 fusion.279
  489.8 1.7 fusion.279
  494.9 14.6 %all-gather.8 = bf16[128,8,3]{1,2,0:T(4,128)(2,1)S(1)} all-gather(bf16[16,8,3]{1,2,0:T(4,128)(2,1)S(1)} %copy.330), channel_id=10, replica_groups=mesh['seq'=8,'req'=32] {'seq'}, dimensions={0}, use_global_device_ids=true | all-gather | bytes 6912 | tf_op jit(solution)/shard_map/all_gather | solution.py:18
  512.0 14.6 %all-gather.9 = bf16[128,8,3]{1,2,0:T(4,128)(2,1)S(1)} all-gather(bf16[16,8,3]{1,2,0:T(4,128)(2,1)S(1)} %copy.331), channel_id=11, replica_groups=mesh['seq'=8,'req'=32] {'seq'}, dimensions={0}, use_global_device_ids=true | all-gather | bytes 6912 | tf_op jit(solution)/shard_map/all_gather | solution.py:18
  529.8 15.5 %all-gather.10 = bf16[128,8,3,64]{3,0,2,1:T(8,128)(2,1)S(1)} all-gather(bf16[16,8,3,64]{3,0,2,1:T(8,128)(2,1)S(1)} %fusion.86), channel_id=12, replica_groups=mesh['seq'=8,'req'=32] {'seq'}, dimensions={0}, use_global_device_ids=true | all-gather | bytes 442368 | tf_op jit(solution)/shard_map/all_gather | solution.py:18
  549.6 33.8 %while.86 = (s32[]{:T(128)}, f32[16,8,3]{0,1,2:T(8,128)S(1)}, f32[16,8,3]{0,1,2:T(8,128)S(1)}, f32[16,8,3,64]{3,2,1,0:T(4,128)S(1)}, bf16[8,16,8,3]{1,2,3,0:T(8,...) while((s32[]{:T(128)}, f32[16,8,3]{0,1,2:T(8,128)S(1)}, ...), condition=%wide.region_26.29_spmd, body=%wide.region_25.28_spmd.sunk | while | flops 101381 | bytes 364183 | solution.py:30
  585.4 2.0 convolution_convert_fusion.2
  587.3 1.9 convolution_convert_fusion.3
  590.0 14.6 %all-gather.5 = bf16[128,8,3]{1,2,0:T(4,128)(2,1)S(1)} all-gather(bf16[16,8,3]{1,2,0:T(4,128)(2,1)S(1)} %copy.310), channel_id=7, replica_groups=mesh['seq'=8,'req'=32] {'seq'}, dimensions={0}, use_global_device_ids=true | all-gather | bytes 6912 | tf_op jit(solution)/shard_map/all_gather | solution.py:18
  607.1 14.6 %all-gather.6 = bf16[128,8,3]{1,2,0:T(4,128)(2,1)S(1)} all-gather(bf16[16,8,3]{1,2,0:T(4,128)(2,1)S(1)} %copy.311), channel_id=8, replica_groups=mesh['seq'=8,'req'=32] {'seq'}, dimensions={0}, use_global_device_ids=true | all-gather | bytes 6912 | tf_op jit(solution)/shard_map/all_gather | solution.py:18
  624.9 15.8 %all-gather.7 = bf16[128,8,3,64]{3,0,2,1:T(8,128)(2,1)S(1)} all-gather(bf16[16,8,3,64]{3,0,2,1:T(8,128)(2,1)S(1)} %fusion.85), channel_id=9, replica_groups=mesh['seq'=8,'req'=32] {'seq'}, dimensions={0}, use_global_device_ids=true | all-gather | bytes 442368 | tf_op jit(solution)/shard_map/all_gather | solution.py:18
  645.0 33.6 %while.85 = (s32[]{:T(128)}, f32[16,8,3]{0,1,2:T(8,128)S(1)}, f32[16,8,3]{0,1,2:T(8,128)S(1)}, f32[16,8,3,64]{3,2,1,0:T(4,128)S(1)}, bf16[8,16,8,3]{1,2,3,0:T(8,...) while((s32[]{:T(128)}, f32[16,8,3]{0,1,2:T(8,128)S(1)}, ...), condition=%wide.region_17.20_spmd, body=%wide.region_16.19_spmd.sunk | while | flops 101381 | bytes 364183 | solution.py:30
  680.6 1.9 convolution_convert_fusion.4
  683.3 14.6 %all-gather.1 = bf16[128,8,3]{1,2,0:T(4,128)(2,1)S(1)} all-gather(bf16[16,8,3]{1,2,0:T(4,128)(2,1)S(1)} %copy.285), channel_id=3, replica_groups=mesh['seq'=8,'req'=32] {'seq'}, dimensions={0}, use_global_device_ids=true | all-gather | bytes 6912 | tf_op jit(solution)/shard_map/all_gather | solution.py:18
  700.5 14.6 %all-gather.2 = bf16[128,8,3]{1,2,0:T(4,128)(2,1)S(1)} all-gather(bf16[16,8,3]{1,2,0:T(4,128)(2,1)S(1)} %copy.286), channel_id=4, replica_groups=mesh['seq'=8,'req'=32] {'seq'}, dimensions={0}, use_global_device_ids=true | all-gather | bytes 6912 | tf_op jit(solution)/shard_map/all_gather | solution.py:18
  718.2 15.5 %all-gather.4 = bf16[128,8,3,64]{3,0,2,1:T(8,128)(2,1)S(1)} all-gather(bf16[16,8,3,64]{3,0,2,1:T(8,128)(2,1)S(1)} %fusion.84), channel_id=6, replica_groups=mesh['seq'=8,'req'=32] {'seq'}, dimensions={0}, use_global_device_ids=true | all-gather | bytes 442368 | tf_op jit(solution)/shard_map/all_gather | solution.py:18
  738.0 33.7 %while.84 = (s32[]{:T(128)}, f32[16,8,3]{0,1,2:T(8,128)S(1)}, f32[16,8,3]{0,1,2:T(8,128)S(1)}, f32[16,8,3,64]{3,2,1,0:T(4,128)S(1)}, bf16[8,16,8,3]{1,2,3,0:T(8,...) while((s32[]{:T(128)}, f32[16,8,3]{0,1,2:T(8,128)S(1)}, ...), condition=%wide.region_8.11_spmd, body=%wide.region_7.10_spmd.sunk | while | flops 101381 | bytes 364183 | solution.py:30
  773.6 1.9 convolution_convert_fusion.5
  776.5 72.4 %all-reduce.7.cloned.1.call-done = (bf16[16,1536]{1,0:T(8,128)(2,1)}, bf16[16,1536]{1,0:T(8,128)(2,1)}, bf16[16,1536]{1,0:T(8,128)(2,1)}, bf16[16,1536]{1,0:T(8,128)(2,1)}) async-done(((bf16[16,1536]{1,0:T(8,128)(2,1)}, bf16[16,1536]{1,0:T(8,128)(2,1)}, bf16[16,1536]{1,0:T(8,128)(2,1)}, bf16[16,1536]{1,0:T(8,128)(2,1)}), (bf16[16,1536]{1,0:T(8,128)(2,1)}, bf16[16,1536]{1,0:T(8,128)(2,1)}, ...) | async-done | bytes 196624
  853.5 16.4 %all_to_all.46 = bf16[32,1,4,1536]{3,2,1,0:T(4,128)(2,1)S(1)} all-to-all(bf16[32,1,4,1536]{3,2,1,0:T(4,128)(2,1)} %bitcast.395), channel_id=1, replica_groups=mesh['seq'=8,'req'=32] {'req'}, dimensions={0} | all-to-all | bytes 786432 | tf_op jit(solution)/shard_map/all_to_all | solution.py:214
  871.9 4.8 all-to-all-start.3
  881.5 3.9 all-to-all-done.3
  (496 shorter events, 267.2 us)
Async XLA Ops:
  7.2 862.7 %copy-start = (bf16[1,1536,1024]{2,1,0:T(8,128)(2,1)S(1)}, bf16[1,1536,1024]{2,1,0:T(8,128)(2,1)}, u32[]{:S(2)}) copy-start(bf16[1,1536,1024]{2,1,0:T(8,128)(2,1)} %param.58) | copy-start | bytes 9437188
  7.2 156.3 %copy-start.26 = (bf16[1,2,4,1536]{3,2,1,0:T(4,128)(2,1)S(1)}, bf16[1,2,4,1536]{3,2,1,0:T(4,128)(2,1)}, u32[]{:S(2)}) copy-start(bf16[1,2,4,1536]{3,2,1,0:T(4,128)(2,1)} %param.45) | copy-start | bytes 73732
  29.6 242.2 %all-to-all-start = ((bf16[8,2,256]{2,1,0:T(2,128)(2,1)}), bf16[8,2,256]{2,1,0:T(2,128)(2,1)}, u32[]{:S(2)}, u32[]{:S(2)}) async-start(bf16[8,2,256]{2,1,0:T(2,128)(2,1)} %reshape.1151), calls=%async_computation | async-start | bytes 16384 | tf_op jit(solution)/shard_map/all_to_all | solution.py:190
  38.5 69.6 %copy-start.63 = (pred[2]{0:T(512)(128)(4,1)}, pred[2]{0:T(512)(128)(4,1)S(1)}, u32[]{:S(2)}) copy-start(pred[2]{0:T(512)(128)(4,1)S(1)} %get-tuple-element.1064) | copy-start | bytes 10
  38.5 149.1 %copy-start.61 = (pred[2]{0:T(512)(128)(4,1)}, pred[2]{0:T(512)(128)(4,1)S(1)}, u32[]{:S(2)}) copy-start(pred[2]{0:T(512)(128)(4,1)S(1)} %get-tuple-element.1060) | copy-start | bytes 10
  38.5 149.1 %copy-start.62 = (pred[2]{0:T(512)(128)(4,1)}, pred[2]{0:T(512)(128)(4,1)S(1)}, u32[]{:S(2)}) copy-start(pred[2]{0:T(512)(128)(4,1)S(1)} %get-tuple-element.1062) | copy-start | bytes 10
  38.5 69.5 %copy-start.59 = (s32[1024]{0:T(1024)}, s32[1024]{0:T(1024)S(1)}, u32[]{:S(2)}) copy-start(s32[1024]{0:T(1024)S(1)} %pad_clamp_fusion.3) | copy-start | bytes 12292
  75.9 89.8 %copy-start.27 = (bf16[2,16,512]{2,1,0:T(8,128)(2,1)}, bf16[2,16,512]{2,1,0:T(8,128)(2,1)S(1)}, u32[]{:S(2)}) copy-start(bf16[2,16,512]{2,1,0:T(8,128)(2,1)S(1)} %get-tuple-element.1074) | copy-start | bytes 98308
  92.3 18.7 %copy-start.57 = (s32[1024]{0:T(1024)}, s32[1024]{0:T(1024)S(1)}, u32[]{:S(2)}) copy-start(s32[1024]{0:T(1024)S(1)} %pad_clamp_fusion.2) | copy-start | bytes 12292
  111.2 54.5 %copy-start.29 = (bf16[2,16,512]{2,1,0:T(8,128)(2,1)}, bf16[2,16,512]{2,1,0:T(8,128)(2,1)S(1)}, u32[]{:S(2)}) copy-start(bf16[2,16,512]{2,1,0:T(8,128)(2,1)S(1)} %get-tuple-element.1072) | copy-start | bytes 98308
  127.6 18.7 %copy-start.56 = (s32[1024]{0:T(1024)}, s32[1024]{0:T(1024)S(1)}, u32[]{:S(2)}) copy-start(s32[1024]{0:T(1024)S(1)} %pad_clamp_fusion.1) | copy-start | bytes 12292
  191.2 17.9 %copy-start.31 = (bf16[2,16,512]{2,1,0:T(8,128)(2,1)S(1)}, bf16[2,16,512]{2,1,0:T(8,128)(2,1)}, u32[]{:S(2)}) copy-start(bf16[2,16,512]{2,1,0:T(8,128)(2,1)} %get-tuple-element.1070) | copy-start | bytes 98308
  193.5 15.5 %copy-start.65 = (s32[1,16]{1,0:T(1,128)S(1)}, s32[1,16]{1,0:T(1,128)}, u32[]{:S(2)}) copy-start(s32[1,16]{1,0:T(1,128)} %param.47) | copy-start | bytes 196
  193.5 34.8 %copy-start.60 = (pred[2]{0:T(512)(128)(4,1)S(1)}, pred[2]{0:T(512)(128)(4,1)}, u32[]{:S(2)}) copy-start(pred[2]{0:T(512)(128)(4,1)} %get-tuple-element.1032) | copy-start | bytes 10
  196.4 68.7 %copy-start.34 = (bf16[2,4,512]{2,1,0:T(4,128)(2,1)}, bf16[2,4,512]{2,1,0:T(4,128)(2,1)S(1)}, u32[]{:S(2)}) copy-start(bf16[2,4,512]{2,1,0:T(4,128)(2,1)S(1)} %broadcast_select_fusion.14) | copy-start | bytes 24580
  198.1 31.0 %copy-start.73 = (s32[2]{0:T(128)S(1)}, s32[2]{0:T(128)}, u32[]{:S(2)}) copy-start(s32[2]{0:T(128)} %iota_add_fusion) | copy-start | bytes 28
  198.8 29.5 %copy-start.58 = (s32[1024]{0:T(1024)}, s32[1024]{0:T(1024)S(1)}, u32[]{:S(2)}) copy-start(s32[1024]{0:T(1024)S(1)} %pad_clamp_fusion) | copy-start | bytes 12292
  228.4 41.4 %copy-start.32 = (bf16[2,16,512]{2,1,0:T(8,128)(2,1)}, bf16[2,16,512]{2,1,0:T(8,128)(2,1)S(1)}, u32[]{:S(2)}) copy-start(bf16[2,16,512]{2,1,0:T(8,128)(2,1)S(1)} %get-tuple-element.1068) | copy-start | bytes 98308
  229.3 30.6 %copy-start.37 = (pred[16,32]{1,0:T(8,128)(4,1)}, pred[16,32]{1,0:T(8,128)(4,1)S(1)}, u32[]{:S(2)}) copy-start(pred[16,32]{1,0:T(8,128)(4,1)S(1)} %iota_compare_fusion.6) | copy-start | bytes 1540
  231.6 9.2 %copy-start.11 = (bf16[16,8,3,64]{3,2,1,0:T(4,128)(2,1)}, bf16[16,8,3,64]{3,2,1,0:T(4,128)(2,1)S(1)}, u32[]{:S(2)}) copy-start(bf16[16,8,3,64]{3,2,1,0:T(4,128)(2,1)S(1)} %reshape_squeeze.24) | copy-start | bytes 147460
  231.6 4.7 copy-start.1
  236.3 3.0 copy-start.49
  236.3 4.5 copy-start.46
  244.5 8.9 copy-start.12
  244.5 4.7 copy-start.47
  253.4 10.3 %copy-start.30 = (bf16[2,16,512]{2,1,0:T(8,128)(2,1)S(1)}, bf16[2,16,512]{2,1,0:T(8,128)(2,1)}, u32[]{:S(2)}) copy-start(bf16[2,16,512]{2,1,0:T(8,128)(2,1)} %copy-done.29) | copy-start | bytes 98308
  253.4 11.0 %copy-start.28 = (bf16[2,16,512]{2,1,0:T(8,128)(2,1)S(1)}, bf16[2,16,512]{2,1,0:T(8,128)(2,1)}, u32[]{:S(2)}) copy-start(bf16[2,16,512]{2,1,0:T(8,128)(2,1)} %copy-done.27) | copy-start | bytes 98308
  255.0 4.9 copy-start.13
  255.1 4.9 copy-start.48
  255.1 6.3 copy-start.64
  255.1 6.6 copy-start.66
  255.1 6.6 copy-start.67
  255.1 6.6 copy-start.68
  255.1 6.6 copy-start.69
  255.1 6.6 copy-start.70
  255.1 10.0 %copy-start.53 = (bf16[16,4,64]{2,0,1:T(8,128)(2,1)S(1)}, bf16[16,4,64]{2,0,1:T(8,128)(2,1)}, u32[]{:S(2)}) copy-start(bf16[16,4,64]{2,0,1:T(8,128)(2,1)} %convolution_convert_fusion.6) | copy-start | bytes 24580
  259.9 10.6 %copy-start.72 = (u32[256]{0:T(256)S(1)}, u32[256]{0:T(256)}, u32[]{:S(2)}) copy-start(u32[256]{0:T(256)} %constant.478) | copy-start | bytes 3076
  262.4 117.7 %copy-start.51 = (pred[16,8]{0,1:T(8,128)(4,1)}, pred[16,8]{0,1:T(8,128)(4,1)S(1)}, u32[]{:S(2)}) copy-start(pred[16,8]{0,1:T(8,128)(4,1)S(1)} %get-tuple-element.1085) | copy-start | bytes 388
  265.1 12.5 %copy-start.36 = (bf16[2,4,512]{2,1,0:T(4,128)(2,1)S(1)}, bf16[2,4,512]{2,1,0:T(4,128)(2,1)}, u32[]{:S(2)}) copy-start(bf16[2,4,512]{2,1,0:T(4,128)(2,1)} %copy-done.34) | copy-start | bytes 24580
  265.1 30.3 %copy-start.35 = (bf16[2,4,512]{2,1,0:T(4,128)(2,1)S(1)}, bf16[2,4,512]{2,1,0:T(4,128)(2,1)}, u32[]{:S(2)}) copy-start(bf16[2,4,512]{2,1,0:T(4,128)(2,1)} %copy-done.34) | copy-start | bytes 24580
  265.1 112.8 %copy-start.52 = (pred[16,8]{0,1:T(8,128)(4,1)S(1)}, pred[16,8]{0,1:T(8,128)(4,1)}, u32[]{:S(2)}) copy-start(pred[16,8]{0,1:T(8,128)(4,1)} %get-tuple-element.1083) | copy-start | bytes 388
  265.9 118.1 %copy-start.43 = (f32[16,8,3]{0,2,1:T(4,128)S(1)}, f32[16,8,3]{0,2,1:T(4,128)}, u32[]{:S(2)}) copy-start(f32[16,8,3]{0,2,1:T(4,128)} %get-tuple-element.1088) | copy-start | bytes 4612
  265.9 119.4 %copy-start.45 = (f32[16,8,3]{0,2,1:T(4,128)S(1)}, f32[16,8,3]{0,2,1:T(4,128)}, u32[]{:S(2)}) copy-start(f32[16,8,3]{0,2,1:T(4,128)} %get-tuple-element.1106) | copy-start | bytes 4612
  271.8 22.9 %all-to-all-start.1 = ((bf16[8,2,256]{2,1,0:T(2,128)(2,1)}), bf16[8,2,256]{2,1,0:T(2,128)(2,1)S(1)}, u32[]{:S(2)}, u32[]{:S(2)}) async-start(bf16[8,2,256]{2,1,0:T(2,128)(2,1)} %reshape.1153), calls=%async_computation.1 | async-start | bytes 16384 | tf_op jit(solution)/shard_map/all_to_all | solution.py:191
  276.7 572.2 %all-reduce.7.cloned.1.call-start = ((), (), s32[]{:S(2)}) async-start(), calls=%async_computation.4 | async-start | bytes 393216
  377.8 7.4 copy-start.40
  381.9 8.7 copy-start.5
  381.9 8.7 copy-start.10
  386.6 28.8 %copy-start.25 = (f32[16,8,3]{0,2,1:T(4,128)}, f32[16,8,3]{0,2,1:T(4,128)S(1)}, u32[]{:S(2)}) copy-start(f32[16,8,3]{0,2,1:T(4,128)S(1)} %get-tuple-element.1029) | copy-start | bytes 4612
  390.6 1.5 copy-start.44
  390.6 1.5 copy-start.55
  390.6 2.1 copy-start.4
  390.6 4.1 copy-start.3
  392.1 2.1 copy-start.42
  392.1 2.1 copy-start.54
  392.1 2.7 copy-start.2
  392.7 22.7 %copy-start.24 = (f32[16,8,3]{0,2,1:T(4,128)}, f32[16,8,3]{0,2,1:T(4,128)S(1)}, u32[]{:S(2)}) copy-start(f32[16,8,3]{0,2,1:T(4,128)S(1)} %get-tuple-element.1027) | copy-start | bytes 4612
  394.8 20.6 %copy-start.23 = (f32[16,8,3]{0,2,1:T(4,128)}, f32[16,8,3]{0,2,1:T(4,128)S(1)}, u32[]{:S(2)}) copy-start(f32[16,8,3]{0,2,1:T(4,128)S(1)} %get-tuple-element.1025) | copy-start | bytes 4612
  397.8 17.6 %copy-start.14 = (f32[16,8,3,32]{3,0,2,1:T(8,128)S(1)}, f32[16,8,3,32]{3,0,2,1:T(8,128)}, u32[]{:S(2)}) copy-start(f32[16,8,3,32]{3,0,2,1:T(8,128)} %get-tuple-element.1097) | copy-start | bytes 147460
  397.8 17.6 %copy-start.38 = (pred[16,32]{1,0:T(8,128)(4,1)S(1)}, pred[16,32]{1,0:T(8,128)(4,1)}, u32[]{:S(2)}) copy-start(pred[16,32]{1,0:T(8,128)(4,1)} %copy-done.37) | copy-start | bytes 1540
  853.5 17.0 %copy-start.71 = (bf16[1,512,1536]{2,1,0:T(8,128)(2,1)S(1)}, bf16[1,512,1536]{2,1,0:T(8,128)(2,1)}, u32[]{:S(2)}) copy-start(bf16[1,512,1536]{2,1,0:T(8,128)(2,1)} %param.59) | copy-start | bytes 4718596
  870.4 9.0 %copy-start.39 = (bf16[2,4,512]{2,1,0:T(4,128)(2,1)S(1)}, bf16[2,4,512]{2,1,0:T(4,128)(2,1)}, u32[]{:S(2)}) copy-start(bf16[2,4,512]{2,1,0:T(4,128)(2,1)} %scatter.39) | copy-start | bytes 24580
  870.4 9.0 %copy-start.41 = (bf16[2,4,512]{2,1,0:T(4,128)(2,1)S(1)}, bf16[2,4,512]{2,1,0:T(4,128)(2,1)}, u32[]{:S(2)}) copy-start(bf16[2,4,512]{2,1,0:T(4,128)(2,1)} %copy-done.40) | copy-start | bytes 24580
  871.9 13.6 %all-to-all-start.3 = ((bf16[32,1,4,1536]{3,2,1,0:T(4,128)(2,1)}), bf16[32,1,4,1536]{3,2,1,0:T(4,128)(2,1)S(1)}, u32[]{:S(2)}, u32[]{:S(2)}) async-start(bf16[32,1,4,1536]{3,2,1,0:T(4,128)(2,1)} %copy.366), calls=%async_computation.3 | async-start | bytes 786432 | tf_op jit(solution)/shard_map/all_to_all | solution.py:212
  (14 other events, 11.2 us)
Sparse Core Ops, SparseCore 0:
  775.7 73.1 all-reduce.6
where the time goes:
time: 908 us; the launch traced here: 895 us
  blocking collectives  452 us (50%)
  local copies, waits for them, and re-layouts  168 us (19%)
  other arithmetic  103 us (11%)
  waiting for transfers between devices  76.4 us (8%)
  matrix products  64.6 us (7%)
  between operations  15.8 us (2%)
  starting transfers between devices  14.6 us (2%)
    all_gather x12, blocking collectives, merged(): lax.all_gather(a.astype(kind), axis)  179 us
    unnamed x2, waiting for transfers between devices  72.4 us
    all_gather x4, blocking collectives, local(): lax.all_gather(beam_value_cache, 'seq', axis=0, tiled=True)  65.9 us
    all_gather x4, blocking collectives, local(): lax.all_gather(beam_key_cache, 'seq', axis=0, tiled=True)  63.1 us
    add x28, other arithmetic, join_partials(): first_scale[..., None] * first_part[2]  46.6 us
    all_gather x3, blocking collectives, local(): lax.all_gather(newest_key, 'seq', axis=0, tiled=True)  46 us
    all_gather x3, blocking collectives, local(): lax.all_gather(newest_value, 'seq', axis=0, tiled=True)  43.7 us
    dot_general x12, matrix products, local_partial(): jnp.einsum('bgjd,kgd->bgjk', decode_query_step, shaped_keys, preferred_el...  29.1 us
  transfers between devices with their start and end apart: 4, of which 2 were waited for; matrix products, arithmetic and copies ran while one was open for 10% of the time, Pallas kernels for 0%

commit v1 on v0

--- a/solution.py
+++ b/solution.py
@@ -230,7 +230,10 @@
             lax.all_gather(beam_key_cache, "seq", axis=0, tiled=True),
             lax.all_gather(beam_value_cache, "seq", axis=0, tiled=True),
             lax.all_gather(newest_key, "seq", axis=0, tiled=True),
-            lax.all_gather(newest_value, "seq", axis=0, tiled=True),
+            jnp.concatenate(
+                lax.all_to_all(jnp.stack([newest_value] * lax.axis_size("seq")), "seq", 0, 0),
+                axis=0,
+            ),
         )
         beam_key_cache = jnp.take(received[0], chosen_rows, axis=0)
         beam_value_cache = jnp.take(received[1], chosen_rows, axis=0)

time: 908 us -> 930 us (1.024)
  blocking collectives: 452 us -> 416 us
  other arithmetic: 103 us -> 128 us
  local copies, waits for them, and re-layouts: 168 us -> 189 us
  starting transfers between devices: 14.6 us -> 29 us
    all_gather x3 -> x0, blocking collectives: 43.7 us -> none  [local(): lax.all_gather(newest_value, 'seq', axis=0, tiled=True)]
    all_to_all x0 -> x3, starting transfers between devices: none -> 14.4 us  [local(): lax.all_to_all(jnp.stack([newest_value] * lax.axis_size('seq')), 'seq', 0...]
    unnamed x158 -> x154, local copies, waits for them, and re-layouts: 21.2 us -> 21.8 us
  transfers between devices with their start and end apart: 4 -> 7, of which waited for: 2 -> 2; matrix products, arithmetic and copies ran while one was open for 10% -> 15% of each run, Pallas kernels for 0% -> 0%
where the time goes in v1:
time: 930 us; the launch traced here: 917 us
  blocking collectives  416 us (45%)
  local copies, waits for them, and re-layouts  189 us (20%)
  other arithmetic  128 us (14%)
  waiting for transfers between devices  76.6 us (8%)
  matrix products  62.6 us (7%)
  starting transfers between devices  29 us (3%)
  between operations  15.8 us (2%)
    all_gather x12, blocking collectives, merged(): lax.all_gather(a.astype(kind), axis)  186 us
    unnamed x2, waiting for transfers between devices  72.7 us
    all_gather x4, blocking collectives, local(): lax.all_gather(beam_value_cache, 'seq', axis=0, tiled=True)  65.9 us
    all_gather x4, blocking collectives, local(): lax.all_gather(beam_key_cache, 'seq', axis=0, tiled=True)  63.1 us
    add x28, other arithmetic, join_partials(): first_scale[..., None] * first_part[2]  54.4 us
    all_gather x3, blocking collectives, local(): lax.all_gather(newest_key, 'seq', axis=0, tiled=True)  46.1 us
    add x28, other arithmetic, join_partials(): denominator = first_scale * first_part[1] + second_scale * second_part[1]  28.7 us
    dot_general x12, matrix products, local_partial(): jnp.einsum('bgjd,kgd->bgjk', decode_query_step, shaped_keys, preferred_el...  28.4 us
  transfers between devices with their start and end apart: 7, of which 2 were waited for; matrix products, arithmetic and copies ran while one was open for 15% of the time, Pallas kernels for 0%

profile of v1, /device:TPU:8, one launch (start us, length us, event | category | flops | bytes accessed | tf_op | source)
XLA Modules:
  0.0 916.7 jit_solution(4067783848821951426)
XLA Ops:
  9.3 18.2 %all_gather.96 = bf16[16,4,1536]{2,1,0:T(4,128)(2,1)S(1)} all-gather(bf16[2,4,1536]{2,1,0:T(4,128)(2,1)S(1)} %fusion.149), channel_id=1, replica_groups=mesh['seq'=8,'req'=32] {'seq'}, dimensions={0}, use_global_device_ids=true | all-gather | bytes 221184 | tf_op jit(solution)/shard_map/all_gather | solution.py:180
  29.6 4.8 all-to-all-start
  38.4 18.3 %all-gather.3 = bf16[1,16,16,512]{3,2,0,1:T(8,128)(2,1)} all-gather(bf16[1,2,16,512]{3,2,0,1:T(8,128)(2,1)} %bitcast.432), channel_id=5, replica_groups=mesh['seq'=8,'req'=32] {'seq'}, dimensions={1}, use_global_device_ids=true | all-gather | bytes 294912 | tf_op jit(solution)/shard_map/all_gather | solution.py:231
  56.7 16.0 %all-gather = bf16[1,16,16,512]{3,2,0,1:T(8,128)(2,1)} all-gather(bf16[1,2,16,512]{3,2,0,1:T(8,128)(2,1)} %bitcast.433), channel_id=2, replica_groups=mesh['seq'=8,'req'=32] {'seq'}, dimensions={1}, use_global_device_ids=true | all-gather | bytes 294912 | tf_op jit(solution)/shard_map/all_gather | solution.py:230
  75.8 15.7 %all_gather.104 = bf16[16,16,512]{2,1,0:T(8,128)(2,1)} all-gather(bf16[2,16,512]{2,1,0:T(8,128)(2,1)S(1)} %get-tuple-element.1075), channel_id=1, replica_groups=mesh['seq'=8,'req'=32] {'seq'}, dimensions={0}, use_global_device_ids=true | all-gather | bytes 294912 | tf_op jit(solution)/shard_map/all_gather | solution.py:230
  92.2 15.7 %all_gather.108 = bf16[16,16,512]{2,1,0:T(8,128)(2,1)} all-gather(bf16[2,16,512]{2,1,0:T(8,128)(2,1)S(1)} %get-tuple-element.1074), channel_id=1, replica_groups=mesh['seq'=8,'req'=32] {'seq'}, dimensions={0}, use_global_device_ids=true | all-gather | bytes 294912 | tf_op jit(solution)/shard_map/all_gather | solution.py:231
  111.1 15.7 %all_gather.111 = bf16[16,16,512]{2,1,0:T(8,128)(2,1)} all-gather(bf16[2,16,512]{2,1,0:T(8,128)(2,1)S(1)} %get-tuple-element.1073), channel_id=1, replica_groups=mesh['seq'=8,'req'=32] {'seq'}, dimensions={0}, use_global_device_ids=true | all-gather | bytes 294912 | tf_op jit(solution)/shard_map/all_gather | solution.py:230
  127.5 15.7 %all_gather.115 = bf16[16,16,512]{2,1,0:T(8,128)(2,1)} all-gather(bf16[2,16,512]{2,1,0:T(8,128)(2,1)S(1)} %get-tuple-element.1072), channel_id=1, replica_groups=mesh['seq'=8,'req'=32] {'seq'}, dimensions={0}, use_global_device_ids=true | all-gather | bytes 294912 | tf_op jit(solution)/shard_map/all_gather | solution.py:231
  146.9 15.7 %all_gather.118 = bf16[16,16,512]{2,1,0:T(8,128)(2,1)} all-gather(bf16[2,16,512]{2,1,0:T(8,128)(2,1)S(1)} %get-tuple-element.1071), channel_id=1, replica_groups=mesh['seq'=8,'req'=32] {'seq'}, dimensions={0}, use_global_device_ids=true | all-gather | bytes 294912 | tf_op jit(solution)/shard_map/all_gather | solution.py:230
  167.3 20.3 %all_gather.97 = bf16[16,4,1536]{0,1,2:T(4,128)(2,1)S(1)} all-gather(bf16[16,4,192]{0,1,2:T(4,128)(2,1)S(1)} %bitcast.399), channel_id=1, replica_groups=mesh['seq'=8,'req'=32] {'seq'}, dimensions={2}, use_global_device_ids=true | all-gather | bytes 221184 | tf_op jit(solution)/shard_map/all_gather | solution.py:188
  187.6 3.6 fusion.236
  191.1 2.1 copy.352
  205.1 3.9 copy.284
  209.1 16.2 %all_gather.122 = bf16[16,16,512]{2,1,0:T(8,128)(2,1)} all-gather(bf16[2,16,512]{2,1,0:T(8,128)(2,1)S(1)} %copy-done.32), channel_id=1, replica_groups=mesh['seq'=8,'req'=32] {'seq'}, dimensions={0}, use_global_device_ids=true | all-gather | bytes 294912 | tf_op jit(solution)/shard_map/all_gather | solution.py:231
  229.3 2.1 copy.283
  231.6 4.7 bitcast_reduce_fusion
  236.3 3.0 bitcast_reduce_fusion.3
  242.3 2.1 copy.313
  244.6 4.7 bitcast_reduce_fusion.2
  250.8 2.1 copy.333
  253.1 4.7 bitcast_reduce_fusion.1
  257.8 2.3 fusion.247
  266.0 3.9 copy.296
  272.6 4.9 all-to-all-start.1
  279.0 16.9 %all_gather.105 = bf16[16,4,512]{2,1,0:T(4,128)(2,1)S(1)} all-gather(bf16[2,4,512]{2,1,0:T(4,128)(2,1)S(1)} %scatter.26), channel_id=1, replica_groups=mesh['seq'=8,'req'=32] {'seq'}, dimensions={0}, use_global_device_ids=true | all-gather | bytes 73728 | tf_op jit(solution)/shard_map/all_gather | solution.py:232
  298.2 4.8 all-to-all-start.2
  306.1 16.9 %all-gather.1 = bf16[128,8,3]{1,2,0:T(4,128)(2,1)S(1)} all-gather(bf16[16,8,3]{1,2,0:T(4,128)(2,1)S(1)} %copy.294), channel_id=3, replica_groups=mesh['seq'=8,'req'=32] {'seq'}, dimensions={0}, use_global_device_ids=true | all-gather | bytes 6912 | tf_op jit(solution)/shard_map/all_gather | solution.py:18
  325.4 3.3 fusion.72
  329.0 15.6 %all-gather.4 = bf16[128,8,3,64]{3,0,2,1:T(8,128)(2,1)S(1)} all-gather(bf16[16,8,3,64]{3,0,2,1:T(8,128)(2,1)S(1)} %fusion.84), channel_id=6, replica_groups=mesh['seq'=8,'req'=32] {'seq'}, dimensions={0}, use_global_device_ids=true | all-gather | bytes 442368 | tf_op jit(solution)/shard_map/all_gather | solution.py:18
  350.8 14.5 %all_gather.112 = bf16[16,4,512]{2,1,0:T(4,128)(2,1)S(1)} all-gather(bf16[2,4,512]{2,1,0:T(4,128)(2,1)S(1)} %scatter.30), channel_id=1, replica_groups=mesh['seq'=8,'req'=32] {'seq'}, dimensions={0}, use_global_device_ids=true | all-gather | bytes 73728 | tf_op jit(solution)/shard_map/all_gather | solution.py:232
  368.1 4.7 all-to-all-start.3
  376.7 17.1 %all-gather.5 = bf16[128,8,3]{1,2,0:T(4,128)(2,1)S(1)} all-gather(bf16[16,8,3]{1,2,0:T(4,128)(2,1)} %copy.319), channel_id=7, replica_groups=mesh['seq'=8,'req'=32] {'seq'}, dimensions={0}, use_global_device_ids=true | all-gather | bytes 6912 | tf_op jit(solution)/shard_map/all_gather | solution.py:18
  396.6 3.3 fusion.75
  401.1 15.5 %all-gather.7 = bf16[128,8,3,64]{3,0,2,1:T(8,128)(2,1)S(1)} all-gather(bf16[16,8,3,64]{3,0,2,1:T(8,128)(2,1)S(1)} %fusion.85), channel_id=9, replica_groups=mesh['seq'=8,'req'=32] {'seq'}, dimensions={0}, use_global_device_ids=true | all-gather | bytes 442368 | tf_op jit(solution)/shard_map/all_gather | solution.py:18
  424.2 14.6 %all_gather.119 = bf16[16,4,512]{2,1,0:T(4,128)(2,1)S(1)} all-gather(bf16[2,4,512]{2,1,0:T(4,128)(2,1)S(1)} %scatter.34), channel_id=1, replica_groups=mesh['seq'=8,'req'=32] {'seq'}, dimensions={0}, use_global_device_ids=true | all-gather | bytes 73728 | tf_op jit(solution)/shard_map/all_gather | solution.py:232
  441.0 4.8 all-to-all-start.4
  451.1 17.1 %all-gather.8 = bf16[128,8,3]{1,2,0:T(4,128)(2,1)S(1)} all-gather(bf16[16,8,3]{1,2,0:T(4,128)(2,1)} %copy.339), channel_id=10, replica_groups=mesh['seq'=8,'req'=32] {'seq'}, dimensions={0}, use_global_device_ids=true | all-gather | bytes 6912 | tf_op jit(solution)/shard_map/all_gather | solution.py:18
  470.9 3.3 fusion.78
  474.8 15.3 %all-gather.10 = bf16[128,8,3,64]{3,0,2,1:T(8,128)(2,1)S(1)} all-gather(bf16[16,8,3,64]{3,0,2,1:T(8,128)(2,1)S(1)} %fusion.86), channel_id=12, replica_groups=mesh['seq'=8,'req'=32] {'seq'}, dimensions={0}, use_global_device_ids=true | all-gather | bytes 442368 | tf_op jit(solution)/shard_map/all_gather | solution.py:18
  501.7 7.3 fusion.23
  511.8 14.8 %all-gather.11 = bf16[128,8,3]{1,2,0:T(4,128)(2,1)S(1)} all-gather(bf16[16,8,3]{1,2,0:T(4,128)(2,1)} %copy.358), channel_id=13, replica_groups=mesh['seq'=8,'req'=32] {'seq'}, dimensions={0}, use_global_device_ids=true | all-gather | bytes 6912 | tf_op jit(solution)/shard_map/all_gather | solution.py:18
  530.2 2.4 fusion.106
  533.4 14.6 %all-gather.12 = bf16[128,8,3]{1,2,0:T(4,128)(2,1)S(1)} all-gather(bf16[16,8,3]{1,2,0:T(4,128)(2,1)S(1)} %copy.359), channel_id=14, replica_groups=mesh['seq'=8,'req'=32] {'seq'}, dimensions={0}, use_global_device_ids=true | all-gather | bytes 6912 | tf_op jit(solution)/shard_map/all_gather | solution.py:18
  554.4 15.4 %all-gather.13 = bf16[128,8,3,64]{3,0,2,1:T(8,128)(2,1)S(1)} all-gather(bf16[16,8,3,64]{3,0,2,1:T(8,128)(2,1)S(1)} %fusion.87), channel_id=15, replica_groups=mesh['seq'=8,'req'=32] {'seq'}, dimensions={0}, use_global_device_ids=true | all-gather | bytes 442368 | tf_op jit(solution)/shard_map/all_gather | solution.py:18
  574.8 40.3 %while.87 = (s32[]{:T(128)}, f32[16,8,3]{0,1,2:T(8,128)}, f32[16,8,3]{0,1,2:T(8,128)S(1)}, f32[16,8,3,64]{3,2,1,0:T(4,128)}, bf16[8,16,8,3]{1,2,3,0:T(8,128)(2,1...) while((s32[]{:T(128)}, f32[16,8,3]{0,1,2:T(8,128)}, ...), condition=%wide.region_35.38_spmd, body=%wide.region_34.37_spmd.sunk | while | flops 101381 | bytes 364183 | solution.py:30
  584.3 2.0 fusion.279
  595.8 2.0 fusion.279
  618.6 14.8 %all-gather.9 = bf16[128,8,3]{1,2,0:T(4,128)(2,1)S(1)} all-gather(bf16[16,8,3]{1,2,0:T(4,128)(2,1)S(1)} %copy.340), channel_id=11, replica_groups=mesh['seq'=8,'req'=32] {'seq'}, dimensions={0}, use_global_device_ids=true | all-gather | bytes 6912 | tf_op jit(solution)/shard_map/all_gather | solution.py:18
  635.8 36.3 %while.86 = (s32[]{:T(128)}, f32[16,8,3]{0,1,2:T(8,128)S(1)}, f32[16,8,3]{0,1,2:T(8,128)S(1)}, f32[16,8,3,64]{3,2,1,0:T(4,128)}, bf16[8,16,8,3]{1,2,3,0:T(8,128)...) while((s32[]{:T(128)}, f32[16,8,3]{0,1,2:T(8,128)S(1)}, ...), condition=%wide.region_26.29_spmd, body=%wide.region_25.28_spmd.sunk | while | flops 101381 | bytes 364183 | solution.py:30
  638.9 2.0 fusion.277
  644.1 2.0 fusion.277
  649.3 2.0 fusion.277
  654.5 2.0 fusion.277
  659.7 2.0 fusion.277
  664.8 2.0 fusion.277
  670.0 2.0 fusion.277
  679.5 14.6 %all-gather.6 = bf16[128,8,3]{1,2,0:T(4,128)(2,1)S(1)} all-gather(bf16[16,8,3]{1,2,0:T(4,128)(2,1)S(1)} %copy.320), channel_id=8, replica_groups=mesh['seq'=8,'req'=32] {'seq'}, dimensions={0}, use_global_device_ids=true | all-gather | bytes 6912 | tf_op jit(solution)/shard_map/all_gather | solution.py:18
  696.4 40.1 %while.85 = (s32[]{:T(128)}, f32[16,8,3]{0,1,2:T(8,128)}, f32[16,8,3]{0,1,2:T(8,128)S(1)}, f32[16,8,3,64]{3,2,1,0:T(4,128)}, bf16[8,16,8,3]{1,2,3,0:T(8,128)(2,1...) while((s32[]{:T(128)}, f32[16,8,3]{0,1,2:T(8,128)}, ...), condition=%wide.region_17.20_spmd, body=%wide.region_16.19_spmd.sunk | while | flops 101381 | bytes 364183 | solution.py:30
  742.1 14.6 %all-gather.2 = bf16[128,8,3]{1,2,0:T(4,128)(2,1)S(1)} all-gather(bf16[16,8,3]{1,2,0:T(4,128)(2,1)S(1)} %copy.295), channel_id=4, replica_groups=mesh['seq'=8,'req'=32] {'seq'}, dimensions={0}, use_global_device_ids=true | all-gather | bytes 6912 | tf_op jit(solution)/shard_map/all_gather | solution.py:18
  759.0 33.8 %while.84 = (s32[]{:T(128)}, f32[16,8,3]{0,1,2:T(8,128)S(1)}, f32[16,8,3]{0,1,2:T(8,128)S(1)}, f32[16,8,3,64]{3,2,1,0:T(4,128)S(1)}, bf16[8,16,8,3]{1,2,3,0:T(8,...) while((s32[]{:T(128)}, f32[16,8,3]{0,1,2:T(8,128)S(1)}, ...), condition=%wide.region_8.11_spmd, body=%wide.region_7.10_spmd.sunk | while | flops 101381 | bytes 364183 | solution.py:30
  797.7 72.7 %all-reduce.7.cloned.1.call-done = (bf16[16,1536]{1,0:T(8,128)(2,1)}, bf16[16,1536]{1,0:T(8,128)(2,1)}, bf16[16,1536]{1,0:T(8,128)(2,1)}, bf16[16,1536]{1,0:T(8,128)(2,1)}) async-done(((bf16[16,1536]{1,0:T(8,128)(2,1)}, bf16[16,1536]{1,0:T(8,128)(2,1)}, bf16[16,1536]{1,0:T(8,128)(2,1)}, bf16[16,1536]{1,0:T(8,128)(2,1)}), (bf16[16,1536]{1,0:T(8,128)(2,1)}, bf16[16,1536]{1,0:T(8,128)(2,1)}, ...) | async-done | bytes 196624
  874.9 16.4 %all_to_all.62 = bf16[32,1,4,1536]{3,2,1,0:T(4,128)(2,1)S(1)} all-to-all(bf16[32,1,4,1536]{3,2,1,0:T(4,128)(2,1)} %bitcast.398), channel_id=1, replica_groups=mesh['seq'=8,'req'=32] {'req'}, dimensions={0} | all-to-all | bytes 786432 | tf_op jit(solution)/shard_map/all_to_all | solution.py:214
  893.3 4.8 all-to-all-start.6
  903.0 3.9 all-to-all-done.6
  (498 shorter events, 301.8 us)
Async XLA Ops:
  7.2 884.1 %copy-start = (bf16[1,1536,1024]{2,1,0:T(8,128)(2,1)S(1)}, bf16[1,1536,1024]{2,1,0:T(8,128)(2,1)}, u32[]{:S(2)}) copy-start(bf16[1,1536,1024]{2,1,0:T(8,128)(2,1)} %param.58) | copy-start | bytes 9437188
  7.2 156.2 %copy-start.27 = (bf16[1,2,4,1536]{3,2,1,0:T(4,128)(2,1)S(1)}, bf16[1,2,4,1536]{3,2,1,0:T(4,128)(2,1)}, u32[]{:S(2)}) copy-start(bf16[1,2,4,1536]{3,2,1,0:T(4,128)(2,1)} %param.45) | copy-start | bytes 73732
  29.6 243.0 %all-to-all-start = ((bf16[8,2,256]{2,1,0:T(2,128)(2,1)}), bf16[8,2,256]{2,1,0:T(2,128)(2,1)}, u32[]{:S(2)}, u32[]{:S(2)}) async-start(bf16[8,2,256]{2,1,0:T(2,128)(2,1)} %reshape.1170), calls=%async_computation | async-start | bytes 16384 | tf_op jit(solution)/shard_map/all_to_all | solution.py:190
  38.4 69.5 %copy-start.67 = (pred[2]{0:T(512)(128)(4,1)}, pred[2]{0:T(512)(128)(4,1)S(1)}, u32[]{:S(2)}) copy-start(pred[2]{0:T(512)(128)(4,1)S(1)} %get-tuple-element.1064) | copy-start | bytes 10
  38.4 149.1 %copy-start.65 = (pred[2]{0:T(512)(128)(4,1)}, pred[2]{0:T(512)(128)(4,1)S(1)}, u32[]{:S(2)}) copy-start(pred[2]{0:T(512)(128)(4,1)S(1)} %get-tuple-element.1060) | copy-start | bytes 10
  38.4 149.1 %copy-start.66 = (pred[2]{0:T(512)(128)(4,1)}, pred[2]{0:T(512)(128)(4,1)S(1)}, u32[]{:S(2)}) copy-start(pred[2]{0:T(512)(128)(4,1)S(1)} %get-tuple-element.1062) | copy-start | bytes 10
  38.4 69.5 %copy-start.63 = (s32[1024]{0:T(1024)}, s32[1024]{0:T(1024)S(1)}, u32[]{:S(2)}) copy-start(s32[1024]{0:T(1024)S(1)} %pad_clamp_fusion.3) | copy-start | bytes 12292
  75.8 89.8 %copy-start.28 = (bf16[2,16,512]{2,1,0:T(8,128)(2,1)}, bf16[2,16,512]{2,1,0:T(8,128)(2,1)S(1)}, u32[]{:S(2)}) copy-start(bf16[2,16,512]{2,1,0:T(8,128)(2,1)S(1)} %get-tuple-element.1074) | copy-start | bytes 98308
  92.2 18.7 %copy-start.62 = (s32[1024]{0:T(1024)}, s32[1024]{0:T(1024)S(1)}, u32[]{:S(2)}) copy-start(s32[1024]{0:T(1024)S(1)} %pad_clamp_fusion.2) | copy-start | bytes 12292
  111.1 54.5 %copy-start.30 = (bf16[2,16,512]{2,1,0:T(8,128)(2,1)}, bf16[2,16,512]{2,1,0:T(8,128)(2,1)S(1)}, u32[]{:S(2)}) copy-start(bf16[2,16,512]{2,1,0:T(8,128)(2,1)S(1)} %get-tuple-element.1072) | copy-start | bytes 98308
  127.5 18.7 %copy-start.61 = (s32[1024]{0:T(1024)}, s32[1024]{0:T(1024)S(1)}, u32[]{:S(2)}) copy-start(s32[1024]{0:T(1024)S(1)} %pad_clamp_fusion.1) | copy-start | bytes 12292
  191.1 18.0 %copy-start.32 = (bf16[2,16,512]{2,1,0:T(8,128)(2,1)S(1)}, bf16[2,16,512]{2,1,0:T(8,128)(2,1)}, u32[]{:S(2)}) copy-start(bf16[2,16,512]{2,1,0:T(8,128)(2,1)} %get-tuple-element.1070) | copy-start | bytes 98308
  193.4 45.9 %copy-start.8 = (bf16[16,8,3,64]{3,2,1,0:T(4,128)(2,1)}, bf16[16,8,3,64]{3,2,1,0:T(4,128)(2,1)S(1)}, u32[]{:S(2)}) copy-start(bf16[16,8,3,64]{3,2,1,0:T(4,128)(2,1)S(1)} %reshape_squeeze.29) | copy-start | bytes 147460
  193.4 15.6 %copy-start.69 = (s32[1,16]{1,0:T(1,128)S(1)}, s32[1,16]{1,0:T(1,128)}, u32[]{:S(2)}) copy-start(s32[1,16]{1,0:T(1,128)} %param.47) | copy-start | bytes 196
  193.4 34.9 %copy-start.64 = (pred[2]{0:T(512)(128)(4,1)S(1)}, pred[2]{0:T(512)(128)(4,1)}, u32[]{:S(2)}) copy-start(pred[2]{0:T(512)(128)(4,1)} %get-tuple-element.1032) | copy-start | bytes 10
  193.4 35.7 %copy-start.71 = (s32[2]{0:T(128)S(1)}, s32[2]{0:T(128)}, u32[]{:S(2)}) copy-start(s32[2]{0:T(128)} %iota_add_fusion) | copy-start | bytes 28
  196.4 68.2 %copy-start.38 = (bf16[2,4,512]{2,1,0:T(4,128)(2,1)}, bf16[2,4,512]{2,1,0:T(4,128)(2,1)S(1)}, u32[]{:S(2)}) copy-start(bf16[2,4,512]{2,1,0:T(4,128)(2,1)S(1)} %broadcast_select_fusion.14) | copy-start | bytes 24580
  198.8 37.5 %copy-start.60 = (s32[1024]{0:T(1024)}, s32[1024]{0:T(1024)S(1)}, u32[]{:S(2)}) copy-start(s32[1024]{0:T(1024)S(1)} %pad_clamp_fusion) | copy-start | bytes 12292
  209.1 43.9 %copy-start.41 = (pred[2048]{0:T(1024)(128)(4,1)}, pred[2048]{0:T(1024)(128)(4,1)S(1)}, u32[]{:S(2)}) copy-start(pred[2048]{0:T(1024)(128)(4,1)S(1)} %fusion.201) | copy-start | bytes 6148
  228.4 41.5 %copy-start.33 = (bf16[2,16,512]{2,1,0:T(8,128)(2,1)}, bf16[2,16,512]{2,1,0:T(8,128)(2,1)S(1)}, u32[]{:S(2)}) copy-start(bf16[2,16,512]{2,1,0:T(8,128)(2,1)S(1)} %get-tuple-element.1068) | copy-start | bytes 98308
  229.3 28.5 %copy-start.44 = (pred[16,32]{1,0:T(8,128)(4,1)}, pred[16,32]{1,0:T(8,128)(4,1)S(1)}, u32[]{:S(2)}) copy-start(pred[16,32]{1,0:T(8,128)(4,1)S(1)} %iota_compare_fusion.6) | copy-start | bytes 1540
  231.6 9.2 %copy-start.11 = (bf16[16,8,3,64]{3,2,1,0:T(4,128)(2,1)}, bf16[16,8,3,64]{3,2,1,0:T(4,128)(2,1)S(1)}, u32[]{:S(2)}) copy-start(bf16[16,8,3,64]{3,2,1,0:T(4,128)(2,1)S(1)} %reshape_squeeze.24) | copy-start | bytes 147460
  231.6 4.7 copy-start.1
  236.3 4.5 copy-start.53
  242.3 7.0 copy-start.54
  244.6 6.2 copy-start.10
  252.8 7.3 copy-start.68
  252.9 10.2 %copy-start.31 = (bf16[2,16,512]{2,1,0:T(8,128)(2,1)S(1)}, bf16[2,16,512]{2,1,0:T(8,128)(2,1)}, u32[]{:S(2)}) copy-start(bf16[2,16,512]{2,1,0:T(8,128)(2,1)} %copy-done.30) | copy-start | bytes 98308
  252.9 10.9 %copy-start.29 = (bf16[2,16,512]{2,1,0:T(8,128)(2,1)S(1)}, bf16[2,16,512]{2,1,0:T(8,128)(2,1)}, u32[]{:S(2)}) copy-start(bf16[2,16,512]{2,1,0:T(8,128)(2,1)} %copy-done.28) | copy-start | bytes 98308
  253.1 16.8 %copy-start.9 = (bf16[16,8,3,64]{3,2,1,0:T(4,128)(2,1)}, bf16[16,8,3,64]{3,2,1,0:T(4,128)(2,1)S(1)}, u32[]{:S(2)}) copy-start(bf16[16,8,3,64]{3,2,1,0:T(4,128)(2,1)S(1)} %reshape_squeeze.28) | copy-start | bytes 147460
  257.8 46.6 %copy-start.12 = (bf16[16,8,3,64]{3,2,1,0:T(4,128)(2,1)S(1)}, bf16[16,8,3,64]{3,2,1,0:T(4,128)(2,1)}, u32[]{:S(2)}) copy-start(bf16[16,8,3,64]{3,2,1,0:T(4,128)(2,1)} %copy-done.11) | copy-start | bytes 147460
  264.5 14.5 %copy-start.40 = (bf16[2,4,512]{2,1,0:T(4,128)(2,1)S(1)}, bf16[2,4,512]{2,1,0:T(4,128)(2,1)}, u32[]{:S(2)}) copy-start(bf16[2,4,512]{2,1,0:T(4,128)(2,1)} %copy-done.38) | copy-start | bytes 24580
  264.5 32.3 %copy-start.39 = (bf16[2,4,512]{2,1,0:T(4,128)(2,1)S(1)}, bf16[2,4,512]{2,1,0:T(4,128)(2,1)}, u32[]{:S(2)}) copy-start(bf16[2,4,512]{2,1,0:T(4,128)(2,1)} %copy-done.38) | copy-start | bytes 24580
  264.5 40.8 %copy-start.50 = (f32[16,8,3]{0,2,1:T(4,128)S(1)}, f32[16,8,3]{0,2,1:T(4,128)}, u32[]{:S(2)}) copy-start(f32[16,8,3]{0,2,1:T(4,128)} %get-tuple-element.1094) | copy-start | bytes 4612
  272.6 23.5 %all-to-all-start.1 = ((bf16[8,2,256]{2,1,0:T(2,128)(2,1)}), bf16[8,2,256]{2,1,0:T(2,128)(2,1)S(1)}, u32[]{:S(2)}, u32[]{:S(2)}) async-start(bf16[8,2,256]{2,1,0:T(2,128)(2,1)} %reshape.1172), calls=%async_computation.1 | async-start | bytes 16384 | tf_op jit(solution)/shard_map/all_to_all | solution.py:191
  298.2 49.6 %all-to-all-start.2 = ((bf16[8,2,4,512]{3,2,1,0:T(4,128)(2,1)}), bf16[8,2,4,512]{3,2,1,0:T(4,128)(2,1)}, u32[]{:S(2)}, u32[]{:S(2)}) async-start(bf16[8,2,4,512]{3,2,1,0:T(4,128)(2,1)} %stack.17), calls=%async_computation.2 | async-start | bytes 131072 | tf_op jit(solution)/shard_map/all_to_all | solution.py:234
  323.7 5.0 copy-start.13
  323.7 5.0 copy-start.37
  324.4 4.3 copy-start.45
  325.4 21.8 %copy-start.59 = (pred[16,8]{0,1:T(8,128)(4,1)S(1)}, pred[16,8]{0,1:T(8,128)(4,1)}, u32[]{:S(2)}) copy-start(pred[16,8]{0,1:T(8,128)(4,1)} %get-tuple-element.1085) | copy-start | bytes 388
  325.4 24.0 %copy-start.56 = (bf16[2,4,512]{2,1,0:T(4,128)(2,1)S(1)}, bf16[2,4,512]{2,1,0:T(4,128)(2,1)}, u32[]{:S(2)}) copy-start(bf16[2,4,512]{2,1,0:T(4,128)(2,1)} %gather_fusion.4) | copy-start | bytes 24580
  328.7 67.9 %copy-start.42 = (pred[2048]{0:T(1024)(128)(4,1)S(1)}, pred[2048]{0:T(1024)(128)(4,1)}, u32[]{:S(2)}) copy-start(pred[2048]{0:T(1024)(128)(4,1)} %copy-done.41) | copy-start | bytes 6148
  368.1 53.1 %all-to-all-start.3 = ((bf16[8,2,4,512]{3,2,1,0:T(4,128)(2,1)}), bf16[8,2,4,512]{3,2,1,0:T(4,128)(2,1)}, u32[]{:S(2)}, u32[]{:S(2)}) async-start(bf16[8,2,4,512]{3,2,1,0:T(4,128)(2,1)} %stack.19), calls=%async_computation.3 | async-start | bytes 131072 | tf_op jit(solution)/shard_map/all_to_all | solution.py:234
  396.5 3.4 copy-start.52
  396.5 4.2 copy-start.14
  396.5 4.3 copy-start.36
  396.5 26.2 %copy-start.57 = (bf16[2,4,512]{2,1,0:T(4,128)(2,1)S(1)}, bf16[2,4,512]{2,1,0:T(4,128)(2,1)}, u32[]{:S(2)}) copy-start(bf16[2,4,512]{2,1,0:T(4,128)(2,1)} %gather_fusion.8) | copy-start | bytes 24580
  441.0 53.8 %all-to-all-start.4 = ((bf16[8,2,4,512]{3,2,1,0:T(4,128)(2,1)}), bf16[8,2,4,512]{3,2,1,0:T(4,128)(2,1)}, u32[]{:S(2)}, u32[]{:S(2)}) async-start(bf16[8,2,4,512]{3,2,1,0:T(4,128)(2,1)} %stack.21), calls=%async_computation.4 | async-start | bytes 131072 | tf_op jit(solution)/shard_map/all_to_all | solution.py:234
  445.8 424.5 %all-reduce.7.cloned.1.call-start = ((), (), s32[]{:S(2)}) async-start(), calls=%async_computation.7 | async-start | bytes 393216
  470.9 3.4 copy-start.51
  470.9 3.4 copy-start.58
  470.9 3.6 copy-start.15
  470.9 3.6 copy-start.35
  470.9 3.6 copy-start.46
  501.7 7.4 copy-start.24
  501.7 7.4 copy-start.2
  501.7 7.4 copy-start.7
  501.7 7.4 copy-start.43
  574.8 61.0 %copy-start.26 = (f32[16,8,3]{0,1,2:T(8,128)S(1)}, f32[16,8,3]{0,1,2:T(8,128)}, u32[]{:S(2)}) copy-start(f32[16,8,3]{0,1,2:T(8,128)} %copy.345) | copy-start | bytes 4612
  696.4 62.6 %copy-start.25 = (f32[16,8,3]{0,1,2:T(8,128)S(1)}, f32[16,8,3]{0,1,2:T(8,128)}, u32[]{:S(2)}) copy-start(f32[16,8,3]{0,1,2:T(8,128)} %copy.305) | copy-start | bytes 4612
  874.8 17.0 %copy-start.70 = (bf16[1,512,1536]{2,1,0:T(8,128)(2,1)S(1)}, bf16[1,512,1536]{2,1,0:T(8,128)(2,1)}, u32[]{:S(2)}) copy-start(bf16[1,512,1536]{2,1,0:T(8,128)(2,1)} %param.59) | copy-start | bytes 4718596
  891.8 9.1 copy-start.47
  891.8 9.1 copy-start.49
  893.3 13.6 %all-to-all-start.6 = ((bf16[32,1,4,1536]{3,2,1,0:T(4,128)(2,1)}), bf16[32,1,4,1536]{3,2,1,0:T(4,128)(2,1)S(1)}, u32[]{:S(2)}, u32[]{:S(2)}) async-start(bf16[32,1,4,1536]{3,2,1,0:T(4,128)(2,1)} %copy.375), calls=%async_computation.6 | async-start | bytes 786432 | tf_op jit(solution)/shard_map/all_to_all | solution.py:212
  (15 other events, 13.4 us)
Sparse Core Ops, SparseCore 0:
  796.9 73.4 all-reduce.6
